TPU v7x, 32 devices: a whole 2x2x4 slice. The times are simulated.
32 devices in a mesh: rep: 8 (over z, core), fsdp: 4 (over y, x).
Axes of the slice: x: 2, y: 2, z: 4, core: 2. Of those that a mesh axis runs over, the one named last changes fastest.
Arguments:
- hidden_in: bfloat16 [10240, 1536], P(('rep', 'fsdp')), may hold values from -6 to 6
- out_grad: bfloat16 [10240, 1536], P(('rep', 'fsdp')), may hold values from -6 to 6
- doc_lengths: int32 [8, 8], P('rep'), may hold values from 1 to 1024, 1280 in all within a row
- piece_starts: int32 [8, 2], P('rep'), may hold values from 0 to 1024, as said below
- w_query: bfloat16 [1536, 1536], P('fsdp'), may hold values from -0.15625 to 0.15625
- b_query: bfloat16 [1536], P('fsdp'), may hold values from -3 to 3
- w_key: bfloat16 [1536, 256], P('fsdp'), may hold values from -0.15625 to 0.15625
- b_key: bfloat16 [256], P('fsdp'), may hold values from -3 to 3
- w_value: bfloat16 [1536, 256], P('fsdp'), may hold values from -0.15625 to 0.15625
- b_value: bfloat16 [256], P('fsdp'), may hold values from -3 to 3
- w_output: bfloat16 [1536, 1536], P('fsdp'), may hold values from -0.625 to 0.625
- gain_attn: bfloat16 [1536], P('fsdp'), may hold values from 0.5 to 1.5
- w_gate: bfloat16 [1536, 8960], P('fsdp'), may hold values from -0.15625 to 0.15625
- w_up: bfloat16 [1536, 8960], P('fsdp'), may hold values from -0.15625 to 0.15625
- w_down: bfloat16 [8960, 1536], P('fsdp'), may hold values from -0.0625 to 0.0625
- gain_mlp: bfloat16 [1536], P('fsdp'), may hold values from 0.5 to 1.5
Outputs:
- output: float32 [10240, 1536], P(('rep', 'fsdp'))
- grad_input: float32 [10240, 1536], P(('rep', 'fsdp'))
- grad_w_query: float32 [1536, 1536], P('fsdp')
- grad_b_query: float32 [1536], P('fsdp')
- grad_w_key: float32 [1536, 256], P('fsdp')
- grad_b_key: float32 [256], P('fsdp')
- grad_w_value: float32 [1536, 256], P('fsdp')
- grad_b_value: float32 [256], P('fsdp')
- grad_w_output: float32 [1536, 1536], P('fsdp')
- grad_gain_attn: float32 [1536], P('fsdp')
- grad_w_gate: float32 [1536, 8960], P('fsdp')
- grad_w_up: float32 [1536, 8960], P('fsdp')
- grad_w_down: float32 [8960, 1536], P('fsdp')
- grad_gain_mlp: float32 [1536], P('fsdp')
Inputs may be any that keep to these rules, and one draw needn't show every extreme that they name: `doc_lengths`: each row's 8 lengths sum to 1280, and the longest is exactly 1024. `piece_starts`: in each row the starts rise by 256 or more from piece to piece, so pieces never intersect; a piece may run over a document's end.
All inputs are finite; a program needn't handle non-finite values.
Results may differ from a plain program's by a relative error of at most 0.028.
Values may be sent and summed in bfloat16 or wider, within the bound.
A program may use at most 576 MiB of HBM per device.

v0:
```python
import jax
import jax.numpy as jnp
from jax import lax
from jax.sharding import PartitionSpec as P

HEADS = 12
KVH = 2
HDIM = 128
PIECE = 256
epsilon = 1e-06
rope_base = 1000000.0


def row_layout(positions, lengths, starts, piece_len):
    doc_ends = jnp.cumsum(lengths)
    passed = positions[:, None] >= doc_ends[None, :]
    doc_ids = jnp.sum(passed.astype(jnp.int32), axis=1, dtype=jnp.int32)
    offsets = jnp.sum(jnp.where(passed, lengths[None, :], 0), axis=1, dtype=jnp.int32)
    inside = (positions[:, None] >= starts[None, :]) & (
        positions[:, None] < starts[None, :] + piece_len
    )
    labels = jnp.arange(1, starts.shape[0] + 1, dtype=jnp.int32)
    piece_ids = jnp.sum(jnp.where(inside, labels[None, :], 0), axis=1, dtype=jnp.int32)
    return (doc_ids, positions - offsets, piece_ids)


def visible_pairs(query_doc, query_pos, query_piece, key_doc, key_pos, key_piece):
    same_doc = query_doc[:, None] == key_doc[None, :]
    causal = key_pos[None, :] <= query_pos[:, None]
    same_piece = (query_piece[:, None] == key_piece[None, :]) & (query_piece[:, None] > 0)
    return same_doc & (causal | same_piece)


def rope_tables(relative, head_dim):
    halves = jnp.arange(0, head_dim, 2).astype(jnp.float32) / head_dim
    inverse = rope_base ** (-halves)
    angles = relative.astype(jnp.float32)[:, None] * inverse[None, :]
    angles = jnp.concatenate([angles, angles], axis=1)
    return (jnp.cos(angles), jnp.sin(angles))


def rotate(values, cosine, sine):
    half_dim = values.shape[-1] // 2
    turned = jnp.concatenate([-values[..., half_dim:], values[..., :half_dim]], axis=-1)
    return values * cosine[:, None, :] + turned * sine[:, None, :]


def unrotate(grads, cosine, sine):
    half_dim = grads.shape[-1] // 2
    spun = grads * sine[:, None, :]
    turned_back = jnp.concatenate([spun[..., half_dim:], -spun[..., :half_dim]], axis=-1)
    return grads * cosine[:, None, :] + turned_back


def mat_dot(left, right):
    return jnp.dot(left, right, preferred_element_type=jnp.float32)


def dot_right_t(left, right):
    return lax.dot_general(
        left, right, (((1,), (1,)), ((), ())), preferred_element_type=jnp.float32
    )


def dot_left_t(left, right):
    return lax.dot_general(
        left, right, (((0,), (0,)), ((), ())), preferred_element_type=jnp.float32
    )


def local(
    hidden_in,
    out_grad,
    doc_lengths,
    piece_starts,
    w_query,
    b_query,
    w_key,
    b_key,
    w_value,
    b_value,
    w_output,
    gain_attn,
    w_gate,
    w_up,
    w_down,
    gain_mlp,
):
    tok_rows = hidden_in.shape[0]
    model_width = hidden_in.shape[1]
    shard_count = lax.axis_size("fsdp")
    row_len = tok_rows * shard_count
    group_size = HEADS // KVH
    kv_width = KVH * HDIM
    ff_width = w_gate.shape[1]
    score_scale = 1.0 / HDIM**0.5
    local_pos = lax.axis_index("fsdp") * tok_rows + jnp.arange(tok_rows, dtype=jnp.int32)
    row_pos = jnp.arange(row_len, dtype=jnp.int32)
    lengths = doc_lengths[0]
    starts = piece_starts[0]
    query_doc, query_rel, query_piece = row_layout(local_pos, lengths, starts, PIECE)
    key_doc, unused_rel, key_piece = row_layout(row_pos, lengths, starts, PIECE)
    allowed = visible_pairs(query_doc, local_pos, query_piece, key_doc, row_pos, key_piece)
    cosine, sine = rope_tables(query_rel, HDIM)
    (
        query_full,
        key_full,
        value_full,
        output_full,
        query_bias,
        key_bias,
        value_bias,
        attn_gain,
        mlp_gain,
    ) = (
        lax.all_gather(w_query, "fsdp", axis=0, tiled=True),
        lax.all_gather(w_key, "fsdp", axis=0, tiled=True),
        lax.all_gather(w_value, "fsdp", axis=0, tiled=True),
        lax.all_gather(w_output, "fsdp", axis=0, tiled=True),
        lax.all_gather(b_query, "fsdp", axis=0, tiled=True),
        lax.all_gather(b_key, "fsdp", axis=0, tiled=True),
        lax.all_gather(b_value, "fsdp", axis=0, tiled=True),
        lax.all_gather(gain_attn, "fsdp", axis=0, tiled=True),
        lax.all_gather(gain_mlp, "fsdp", axis=0, tiled=True),
    )
    x_float = hidden_in.astype(jnp.float32)
    inv_first = lax.rsqrt(jnp.mean(x_float * x_float, axis=1, keepdims=True) + epsilon)
    unit_first = x_float * inv_first
    gain_first = attn_gain.astype(jnp.float32)
    normed_first = (unit_first * gain_first).astype(jnp.bfloat16)
    query_pre = mat_dot(normed_first, query_full) + query_bias.astype(jnp.float32)
    key_pre = mat_dot(normed_first, key_full) + key_bias.astype(jnp.float32)
    value_pre = mat_dot(normed_first, value_full) + value_bias.astype(jnp.float32)
    query_rot = rotate(query_pre.reshape(tok_rows, HEADS, HDIM), cosine, sine).astype(jnp.bfloat16)
    key_rot = (
        rotate(key_pre.reshape(tok_rows, KVH, HDIM), cosine, sine)
        .astype(jnp.bfloat16)
        .reshape(tok_rows, kv_width)
    )
    value_low = value_pre.astype(jnp.bfloat16)
    keys_row, values_row = (
        lax.all_gather(key_rot, "fsdp", axis=0, tiled=True),
        lax.all_gather(value_low, "fsdp", axis=0, tiled=True),
    )
    query_grouped = query_rot.reshape(tok_rows, KVH, group_size, HDIM)
    keys_grouped = keys_row.reshape(row_len, KVH, HDIM)
    values_grouped = values_row.reshape(row_len, KVH, HDIM)

    def masked_scores():
        raw_scores = (
            jnp.einsum(
                "tgjd,rgd->gjtr", query_grouped, keys_grouped, preferred_element_type=jnp.float32
            )
            * score_scale
        )
        return jnp.where(allowed[None, None], raw_scores, -1e30)

    scores = masked_scores()
    row_peak = jnp.max(scores, axis=3, keepdims=True)
    expo_vals = jnp.exp(scores - row_peak)
    row_total = jnp.sum(expo_vals, axis=3, keepdims=True)
    soft_probs = expo_vals / row_total
    log_total = row_peak + jnp.log(row_total)
    attn_heads = jnp.einsum(
        "gjtr,rgd->tgjd",
        soft_probs.astype(jnp.bfloat16),
        values_grouped,
        preferred_element_type=jnp.float32,
    )
    attn_low = attn_heads.reshape(tok_rows, model_width).astype(jnp.bfloat16)
    mid_state = x_float + mat_dot(attn_low, output_full)
    inv_second = lax.rsqrt(jnp.mean(mid_state * mid_state, axis=1, keepdims=True) + epsilon)
    unit_second = mid_state * inv_second
    gain_second = mlp_gain.astype(jnp.float32)
    normed_second = (unit_second * gain_second).astype(jnp.bfloat16)
    cot_float = out_grad.astype(jnp.float32)
    pieces = (
        lax.all_gather(w_gate, "fsdp", axis=0, tiled=True),
        lax.all_gather(w_up, "fsdp", axis=0, tiled=True),
    )
    columns = normed_second
    gate_val = mat_dot(columns, pieces[0])
    up_val = mat_dot(columns, pieces[1])
    sig_gate = jax.nn.sigmoid(gate_val)
    silu_gate = gate_val * sig_gate
    act_low = (silu_gate * up_val).astype(jnp.bfloat16)
    columns = act_low
    mlp_out = mat_dot(columns, lax.all_gather(w_down, "fsdp", axis=0, tiled=True))
    d_act = dot_right_t(out_grad, lax.all_gather(w_down, "fsdp", axis=0, tiled=True))
    columns = act_low
    down_sums = lax.psum_scatter(
        dot_left_t(columns, out_grad).astype(jnp.bfloat16), "fsdp", scatter_dimension=0, tiled=True
    ).astype(jnp.float32)
    d_gate = (d_act * up_val * sig_gate * (1.0 + gate_val * (1.0 - sig_gate))).astype(jnp.bfloat16)
    d_up = (d_act * silu_gate).astype(jnp.bfloat16)
    pieces = (
        lax.all_gather(w_gate, "fsdp", axis=0, tiled=True),
        lax.all_gather(w_up, "fsdp", axis=0, tiled=True),
    )
    partial_value = dot_right_t(d_gate, pieces[0]) + dot_right_t(d_up, pieces[1])
    columns = normed_second
    mlp_sums = lax.psum_scatter(
        jnp.concatenate([dot_left_t(columns, d_gate), dot_left_t(columns, d_up)], axis=1).astype(
            jnp.bfloat16
        ),
        "fsdp",
        scatter_dimension=0,
        tiled=True,
    ).astype(jnp.float32)
    output = mid_state + mlp_out
    d_gain_second = jnp.sum(partial_value * unit_second, axis=0)
    scaled_second = partial_value * gain_second
    d_mid = cot_float + inv_second * (
        scaled_second - unit_second * jnp.mean(scaled_second * unit_second, axis=1, keepdims=True)
    )
    d_branch_low = d_mid.astype(jnp.bfloat16)
    d_attn_low = dot_right_t(d_branch_low, output_full).astype(jnp.bfloat16)
    d_attn_grouped = d_attn_low.reshape(tok_rows, KVH, group_size, HDIM)
    scores = masked_scores()
    soft_back = jnp.exp(scores - log_total)
    probs_low = soft_back.astype(jnp.bfloat16)
    prob_grad = jnp.einsum(
        "tgjd,rgd->gjtr", d_attn_grouped, values_grouped, preferred_element_type=jnp.float32
    )
    row_delta = jnp.sum(soft_back * prob_grad, axis=3, keepdims=True)
    score_grad = (soft_back * (prob_grad - row_delta)).astype(jnp.bfloat16)
    dquery_rot = (
        jnp.einsum("gjtr,rgd->tgjd", score_grad, keys_grouped, preferred_element_type=jnp.float32)
        * score_scale
    )
    dquery_low = (
        unrotate(dquery_rot.reshape(tok_rows, HEADS, HDIM), cosine, sine)
        .reshape(tok_rows, model_width)
        .astype(jnp.bfloat16)
    )
    key_grad = (
        jnp.einsum("gjtr,tgjd->rgd", score_grad, query_grouped, preferred_element_type=jnp.float32)
        * score_scale
    )
    value_grad = jnp.einsum(
        "gjtr,tgjd->rgd", probs_low, d_attn_grouped, preferred_element_type=jnp.float32
    )
    kv_sums = lax.psum_scatter(
        jnp.concatenate(
            [
                key_grad.reshape(lax.axis_size("fsdp") * tok_rows, kv_width),
                value_grad.reshape(lax.axis_size("fsdp") * tok_rows, kv_width),
            ],
            axis=1,
        ).astype(jnp.bfloat16),
        "fsdp",
        scatter_dimension=0,
        tiled=True,
    ).astype(jnp.float32)
    dkey_low = (
        unrotate(kv_sums[:, :kv_width].reshape(tok_rows, KVH, HDIM), cosine, sine)
        .reshape(tok_rows, kv_width)
        .astype(jnp.bfloat16)
    )
    dvalue_low = kv_sums[:, kv_width:].astype(jnp.bfloat16)
    d_norm_first = (
        dot_right_t(dquery_low, query_full)
        + dot_right_t(dkey_low, key_full)
        + dot_right_t(dvalue_low, value_full)
    )
    attn_sums = lax.psum_scatter(
        jnp.concatenate(
            [
                dot_left_t(normed_first, dquery_low),
                dot_left_t(normed_first, dkey_low),
                dot_left_t(normed_first, dvalue_low),
                dot_left_t(attn_low, d_branch_low),
            ],
            axis=1,
        ).astype(jnp.bfloat16),
        "fsdp",
        scatter_dimension=0,
        tiled=True,
    ).astype(jnp.float32)
    d_gain_first = jnp.sum(d_norm_first * unit_first, axis=0)
    scaled_first = d_norm_first * gain_first
    grad_input = d_mid + inv_first * (
        scaled_first - unit_first * jnp.mean(scaled_first * unit_first, axis=1, keepdims=True)
    )
    bias_query = jnp.sum(dquery_low.astype(jnp.float32), axis=0)
    bias_key = jnp.sum(dkey_low.astype(jnp.float32), axis=0)
    bias_value = jnp.sum(dvalue_low.astype(jnp.float32), axis=0)
    bias_query, bias_key, bias_value, gain_first_sum, gain_second_sum = (
        lax.psum_scatter(bias_query, "fsdp", scatter_dimension=0, tiled=True),
        lax.psum_scatter(bias_key, "fsdp", scatter_dimension=0, tiled=True),
        lax.psum_scatter(bias_value, "fsdp", scatter_dimension=0, tiled=True),
        lax.psum_scatter(d_gain_first, "fsdp", scatter_dimension=0, tiled=True),
        lax.psum_scatter(d_gain_second, "fsdp", scatter_dimension=0, tiled=True),
    )
    (
        attn_sums,
        mlp_sums,
        down_sums,
        bias_query,
        bias_key,
        bias_value,
        gain_first_sum,
        gain_second_sum,
    ) = (
        lax.psum(attn_sums.astype(jnp.bfloat16), "rep").astype(jnp.float32),
        lax.psum(mlp_sums.astype(jnp.bfloat16), "rep").astype(jnp.float32),
        lax.psum(down_sums.astype(jnp.bfloat16), "rep").astype(jnp.float32),
        lax.psum(bias_query.astype(jnp.bfloat16), "rep").astype(jnp.float32),
        lax.psum(bias_key.astype(jnp.bfloat16), "rep").astype(jnp.float32),
        lax.psum(bias_value.astype(jnp.bfloat16), "rep").astype(jnp.float32),
        lax.psum(gain_first_sum.astype(jnp.bfloat16), "rep").astype(jnp.float32),
        lax.psum(gain_second_sum.astype(jnp.bfloat16), "rep").astype(jnp.float32),
    )
    grad_query = attn_sums[:, :model_width]
    grad_key = attn_sums[:, model_width : model_width + kv_width]
    grad_value = attn_sums[:, model_width + kv_width : model_width + 2 * kv_width]
    grad_output = attn_sums[:, model_width + 2 * kv_width :]
    grad_gate = mlp_sums[:, :ff_width]
    grad_up = mlp_sums[:, ff_width:]
    return (
        output,
        grad_input,
        grad_query,
        bias_query,
        grad_key,
        bias_key,
        grad_value,
        bias_value,
        grad_output,
        gain_first_sum,
        grad_gate,
        grad_up,
        down_sums,
        gain_second_sum,
    )


def solution(mesh):
    placed = (
        P(("rep", "fsdp"), None),
        P(("rep", "fsdp"), None),
        P("rep", None),
        P("rep", None),
        P("fsdp", None),
        P("fsdp"),
        P("fsdp", None),
        P("fsdp"),
        P("fsdp", None),
        P("fsdp"),
        P("fsdp", None),
        P("fsdp"),
        P("fsdp", None),
        P("fsdp", None),
        P("fsdp", None),
        P("fsdp"),
    )
    return jax.shard_map(
        local,
        mesh=mesh,
        in_specs=placed,
        out_specs=(
            P(("rep", "fsdp"), None),
            P(("rep", "fsdp"), None),
            P("fsdp", None),
            P("fsdp"),
            P("fsdp", None),
            P("fsdp"),
            P("fsdp", None),
            P("fsdp"),
            P("fsdp", None),
            P("fsdp"),
            P("fsdp", None),
            P("fsdp", None),
            P("fsdp", None),
            P("fsdp"),
        ),
        check_vma=False,
    )
```

profile of v0, /device:TPU:0, one launch (start us, length us, event | category | flops | bytes accessed | tf_op | source)
XLA Modules:
  0.0 2377.3 jit_solution(16772693715200293686)
XLA Ops:
  49.7 18.5 all_gather.49
  71.6 12.9 all_gather.51
  85.5 15.4 all_gather.46
  151.1 242.1 %all-gather.15.cloned.1.call-done = bf16[1536,8960]{1,0:T(8,128)(2,1)} async-done(((bf16[384,8960]{1,0:T(8,128)(2,1)}), bf16[1536,8960]{1,0:T(8,128)(2,1)}) %all-gather.15.cloned.1.call-update) | async-done | bytes 27525136 | tf_op jit(solution)/shard_map/all_gather | solution.py:179
  393.2 17.3 fusion.71
  410.5 231.5 %all-gather.13.cloned.1.call-done = bf16[1536,8960]{1,0:T(8,128)(2,1)} async-done(((bf16[384,8960]{1,0:T(8,128)(2,1)}), bf16[1536,8960]{1,0:T(8,128)(2,1)}) %all-gather.13.cloned.1.call-update) | async-done | bytes 27525136 | tf_op jit(solution)/shard_map/all_gather | solution.py:178
  642.1 17.7 fusion.70
  659.8 231.2 %all-gather.17.cloned.1.call-done = bf16[8960,1536]{1,0:T(8,128)(2,1)} async-done(((bf16[2240,1536]{1,0:T(8,128)(2,1)}), bf16[8960,1536]{1,0:T(8,128)(2,1)}) %all-gather.17.cloned.1.call-update) | async-done | bytes 27525136 | tf_op jit(solution)/shard_map/all_gather | solution.py:188
  890.9 24.7 %multiply_convert_fusion = (bf16[320,8960]{1,0:T(8,128)(2,1)}, bf16[320,8960]{1,0:T(8,128)(2,1)}, bf16[320,8960]{1,0:T(8,128)(2,1)}) fusion(f32[320,8960]{1,0:T(8,128)} %fusion.70, f32[320,8960]{1,0:T(8,128)} %fusion.71, bf16[320,1536]{1,0:T(8,128)(2,1)S(1)} %copy-done.33, bf16[8960,1536]{1,0:T(8,128)(2,1)} %all-gather.17.cloned.1.call-done), kind=kOutput, calls=%fused_computation.15 | convolution fusion | flops 8851046400 | bytes 68648960 | tf_op jit(solution)/shard_map/dot_general | solution.py:60
  915.7 16.5 fusion.72
  932.1 17.3 multiply_reduce_fusion
  976.8 13.4 fusion.2
  1039.9 14.6 copy.143
  1054.6 22.4 convolution_convert_fusion.2
  1077.1 21.5 convolution_convert_fusion
  1098.6 21.1 convolution_convert_fusion.1
  1119.7 37.6 %pad_maximum_fusion = bf16[1536,17920]{1,0:T(8,128)(2,1)} fusion(bf16[1536,8960]{1,0:T(8,128)(2,1)} %convolution_convert_fusion, bf16[1536,8960]{1,0:T(8,128)(2,1)} %convolution_convert_fusion.1), kind=kLoop, calls=%fused_computation | loop fusion | flops 110100480 | bytes 110100480 | tf_op jit(solution)/shard_map/concatenate | solution.py:203
  1167.1 239.5 %reduce-scatter.11.cloned.1.call-done = bf16[2240,1536]{1,0:T(8,128)(2,1)} async-done(((bf16[8960,1536]{1,0:T(8,128)(2,1)}), bf16[2240,1536]{1,0:T(8,128)(2,1)}) %reduce-scatter.11.cloned.1.call-update) | async-done | bytes 6881296 | tf_op jit(solution)/shard_map/reduce_scatter | solution.py:191
  1406.6 465.6 %reduce-scatter.9.cloned.1.call-done = bf16[384,17920]{1,0:T(8,128)(2,1)} async-done(((bf16[1536,17920]{1,0:T(8,128)(2,1)}), bf16[384,17920]{1,0:T(8,128)(2,1)}) %reduce-scatter.9.cloned.1.call-update) | async-done | bytes 13762576 | tf_op jit(solution)/shard_map/reduce_scatter | solution.py:202
  1885.8 16.9 convolution_add_fusion.3
  1906.0 15.9 all-reduce.7
  1922.3 14.6 all-reduce.8
  1943.1 392.3 %all-reduce.13.cloned.1.call-done = (bf16[384,3584]{0,1:T(8,128)(2,1)}, bf16[384,17920]{1,0:T(8,128)(2,1)}, bf16[2240,1536]{1,0:T(8,128)(2,1)}) async-done(((bf16[384,3584]{0,1:T(8,128)(2,1)}, bf16[384,17920]{1,0:T(8,128)(2,1)}, bf16[2240,1536]{1,0:T(8,128)(2,1)}), (bf16[384,3584]{0,1:T(8,128)(2,1)}, bf16[384,17920]{1,0:T(8,128)(2,1)}, bf16[2240,1536]{1,0:T(8,128)(2,1)})) %all-reduce.13.cloned.1.call-update) | async-done | bytes 23396368 | tf_op jit(solution)/shard_map/psum | solution.py:305
  2356.7 13.6 fusion.63
  (254 shorter events, 226.0 us)
Async XLA Ops:
  7.2 110.5 %all-gather.9.cloned.1.call-start = ((), (), s32[]{:S(2)}) async-start(), calls=%async_computation.4 | async-start | bytes 5898240 | tf_op jit(solution)/shard_map/all_gather | solution.py:116
  7.9 138.4 %all-gather.11.cloned.1.call-start = ((), (), s32[]{:S(2)}) async-start(), calls=%async_computation.5 | async-start | bytes 5898240 | tf_op jit(solution)/shard_map/all_gather | solution.py:119
  8.7 384.5 %all-gather.15.cloned.1.call-start = ((), (), s32[]{:S(2)}) async-start(), calls=%async_computation.7 | async-start | bytes 34406400 | tf_op jit(solution)/shard_map/all_gather | solution.py:179
  9.4 632.7 %all-gather.13.cloned.1.call-start = ((), (), s32[]{:S(2)}) async-start(), calls=%async_computation.6 | async-start | bytes 34406400 | tf_op jit(solution)/shard_map/all_gather | solution.py:178
  10.0 37.0 %copy-start.52 = (s32[1,8]{1,0:T(1,128)S(1)}, s32[1,8]{1,0:T(1,128)}, u32[]{:S(2)}) copy-start(s32[1,8]{1,0:T(1,128)} %param.18) | copy-start | bytes 100
  10.1 39.6 %copy-start.37 = (bf16[384,256]{1,0:T(8,128)(2,1)S(1)}, bf16[384,256]{1,0:T(8,128)(2,1)}, u32[]{:S(2)}) copy-start(bf16[384,256]{1,0:T(8,128)(2,1)} %param.22) | copy-start | bytes 589828
  10.1 880.9 %all-gather.17.cloned.1.call-start = ((), (), s32[]{:S(2)}) async-start(), calls=%async_computation.8 | async-start | bytes 34406400 | tf_op jit(solution)/shard_map/all_gather | solution.py:188
  10.6 57.6 %copy-start.4 = (bf16[320,1536]{1,0:T(8,128)(2,1)S(1)}, bf16[320,1536]{1,0:T(8,128)(2,1)}, u32[]{:S(2)}) copy-start(bf16[320,1536]{1,0:T(8,128)(2,1)} %param.16) | copy-start | bytes 2949124
  10.7 1014.4 %reduce-scatter.7.cloned.1.call-start = ((), (), s32[]{:S(2)}) async-start(), calls=%async_computation.9 | async-start | bytes 1638400 | tf_op jit(solution)/shard_map/reduce_scatter | solution.py:243
  39.1 78.5 %copy-start.39 = (f32[1536]{0:T(1024)}, f32[1536]{0:T(1024)S(1)}, u32[]{:S(2)}) copy-start(f32[1536]{0:T(1024)S(1)} %reshape.339) | copy-start | bytes 18436
  48.7 21.5 copy-start.23
  48.9 76.8 %copy-start.26 = (f32[320,128]{0,1:T(8,128)}, f32[320,128]{0,1:T(8,128)S(1)}, u32[]{:S(2)}) copy-start(f32[320,128]{0,1:T(8,128)S(1)} %copy.98) | copy-start | bytes 491524
  69.2 48.5 %copy-start.41 = (f32[320]{0:T(512)}, f32[320]{0:T(512)S(1)}, u32[]{:S(2)}) copy-start(f32[320]{0:T(512)S(1)} %add_rsqrt_fusion.1) | copy-start | bytes 3844
  150.8 798.6 %copy-start.2 = (f32[320,1536]{1,0:T(8,128)}, f32[320,1536]{1,0:T(8,128)S(1)}, u32[]{:S(2)}) copy-start(f32[320,1536]{1,0:T(8,128)S(1)} %get-tuple-element.119) | copy-start | bytes 5898244
  151.1 242.1 %copy-start.34 = (bf16[320,1536]{1,0:T(8,128)(2,1)}, bf16[320,1536]{1,0:T(8,128)(2,1)S(1)}, u32[]{:S(2)}) copy-start(bf16[320,1536]{1,0:T(8,128)(2,1)S(1)} %multiply_convert_fusion.3) | copy-start | bytes 2949124
  410.5 480.4 %copy-start.33 = (bf16[320,1536]{1,0:T(8,128)(2,1)S(1)}, bf16[320,1536]{1,0:T(8,128)(2,1)}, u32[]{:S(2)}) copy-start(bf16[320,1536]{1,0:T(8,128)(2,1)} %param.17) | copy-start | bytes 2949124
  915.7 37.1 %slice-start = ((s8[4718592]{0:T(1024)(128)(4,1)}), s8[4194304]{0:T(1024)(128)(4,1)S(1)}, s32[]{:S(2)}) async-start(s8[4718592]{0:T(1024)(128)(4,1)} %bitcast.131), calls=%async_computation.14 | async-start | bytes 8388608
  932.1 20.7 slice-start.1
  995.5 166.9 %reduce-scatter.13.cloned.1.call-start = ((), (), s32[]{:S(2)}) async-start(), calls=%async_computation.12 | async-start | bytes 13762560
  1054.5 352.1 %reduce-scatter.11.cloned.1.call-start = ((), (), s32[]{:S(2)}) async-start(), calls=%async_computation.11 | async-start | bytes 34406400 | tf_op jit(solution)/shard_map/reduce_scatter | solution.py:191
  1077.0 795.2 %reduce-scatter.9.cloned.1.call-start = ((), (), s32[]{:S(2)}) async-start(), calls=%async_computation.10 | async-start | bytes 68812800 | tf_op jit(solution)/shard_map/reduce_scatter | solution.py:202
  1077.1 21.5 copy-start.35
  1157.3 1178.1 %all-reduce.13.cloned.1.call-start = ((), (), s32[]{:S(2)}) async-start(), calls=%async_computation.13 | async-start | bytes 46792704 | tf_op jit(solution)/shard_map/psum | solution.py:305
  1904.0 35.7 %copy-start.10 = (f32[320,1536]{1,0:T(8,128)S(1)}, f32[320,1536]{1,0:T(8,128)}, u32[]{:S(2)}) copy-start(f32[320,1536]{1,0:T(8,128)} %copy-done.8) | copy-start | bytes 5898244
  (43 other events, 213.6 us)
Sparse Core Ops, SparseCore 0:
  9.9 69.6 all-gather.8
  81.4 62.6 all-gather.10
  146.0 247.1 all-gather.14
  394.9 247.1 all-gather.12
  643.8 247.1 all-gather.16
  995.6 29.3 reduce-scatter.6
  1054.6 107.7 reduce-scatter.12
  1165.5 240.9 reduce-scatter.10
  1410.0 462.1 reduce-scatter.8
  1875.5 459.8 all-reduce.12
where the time goes:
time: 2380 us
  waiting for transfers between devices  1810 us (76%)
  matrix products  247 us (10%)
  blocking collectives  124 us (5%)
  other arithmetic  96 us (4%)
  local copies, waits for them, and re-layouts  78.8 us (3%)
    reduce_scatter x1, waiting for transfers between devices, local(): lax.psum_scatter(jnp.concatenate([dot_left_t(columns, d_gate), dot_left_t...  466 us
    psum x1, waiting for transfers between devices, local(): lax.psum(attn_sums.astype(jnp.bfloat16), 'rep').astype(jnp.float32)  392 us
    all_gather x1, waiting for transfers between devices, local(): lax.all_gather(w_up, 'fsdp', axis=0, tiled=True)  242 us
    reduce_scatter x1, waiting for transfers between devices, local(): lax.psum_scatter(dot_left_t(columns, out_grad).astype(jnp.bfloat16), 'fsd...  239 us
    all_gather x1, waiting for transfers between devices, local(): lax.all_gather(w_gate, 'fsdp', axis=0, tiled=True)  232 us
    all_gather x1, waiting for transfers between devices, local(): lax.all_gather(w_down, 'fsdp', axis=0, tiled=True)  231 us
    dot_general x7, matrix products, dot_left_t(): lax.dot_general(left, right, (((0,), (0,)), ((), ())), preferred_element_...  76.4 us
    dot_general x7, matrix products, dot_right_t(): lax.dot_general(left, right, (((1,), (1,)), ((), ())), preferred_element_...  67.8 us
  transfers between devices with their start and end apart: 10, of which 8 were waited for; matrix products, arithmetic and copies ran while one was open for 10% of the time, Pallas kernels for 0%

commit v1 on v0

--- a/solution.py
+++ b/solution.py
@@ -302,7 +302,7 @@
         gain_first_sum,
         gain_second_sum,
     ) = (
-        lax.psum(attn_sums.astype(jnp.bfloat16), "rep").astype(jnp.float32),
+        jnp.sum(lax.all_gather(attn_sums.astype(jnp.bfloat16), "rep"), axis=0).astype(jnp.float32),
         lax.psum(mlp_sums.astype(jnp.bfloat16), "rep").astype(jnp.float32),
         lax.psum(down_sums.astype(jnp.bfloat16), "rep").astype(jnp.float32),
         lax.psum(bias_query.astype(jnp.bfloat16), "rep").astype(jnp.float32),

time: 2380 us -> 2510 us (1.055)
  waiting for transfers between devices: 1810 us -> 1900 us
    all_gather x0 -> x1, waiting for transfers between devices: none -> 124 us  [local(): lax.all_gather(attn_sums.astype(jnp.bfloat16), 'rep')]
    psum x1, waiting for transfers between devices: 392 us -> 354 us  [local(): lax.psum(mlp_sums.astype(jnp.bfloat16), 'rep').astype(jnp.float32)]
    unnamed x133 -> x138, local copies, waits for them, and re-layouts: 41.4 us -> 62.5 us
  transfers between devices with their start and end apart: 10 -> 11, of which waited for: 8 -> 9; matrix products, arithmetic and copies ran while one was open for 10% -> 12% of each run, Pallas kernels for 0% -> 0%
where the time goes in v1:
time: 2510 us; the launch traced here: 2500 us
  waiting for transfers between devices  1900 us (76%)
  matrix products  249 us (10%)
  blocking collectives  124 us (5%)
  other arithmetic  119 us (5%)
  local copies, waits for them, and re-layouts  94.3 us (4%)
    reduce_scatter x1, waiting for transfers between devices, local(): lax.psum_scatter(jnp.concatenate([dot_left_t(columns, d_gate), dot_left_t...  466 us
    psum x1, waiting for transfers between devices, local(): lax.psum(mlp_sums.astype(jnp.bfloat16), 'rep').astype(jnp.float32)  354 us
    all_gather x1, waiting for transfers between devices, local(): lax.all_gather(w_up, 'fsdp', axis=0, tiled=True)  242 us
    reduce_scatter x1, waiting for transfers between devices, local(): lax.psum_scatter(dot_left_t(columns, out_grad).astype(jnp.bfloat16), 'fsd...  239 us
    all_gather x1, waiting for transfers between devices, local(): lax.all_gather(w_gate, 'fsdp', axis=0, tiled=True)  231 us
    all_gather x1, waiting for transfers between devices, local(): lax.all_gather(w_down, 'fsdp', axis=0, tiled=True)  231 us
    all_gather x1, waiting for transfers between devices, local(): lax.all_gather(attn_sums.astype(jnp.bfloat16), 'rep')  124 us
    dot_general x7, matrix products, dot_left_t(): lax.dot_general(left, right, (((0,), (0,)), ((), ())), preferred_element_...  76.4 us
  transfers between devices with their start and end apart: 11, of which 9 were waited for; matrix products, arithmetic and copies ran while one was open for 12% of the time, Pallas kernels for 0%

profile of v1, /device:TPU:0, one launch (start us, length us, event | category | flops | bytes accessed | tf_op | source)
XLA Modules:
  0.0 2503.5 jit_solution(17073849545628568223)
XLA Ops:
  49.7 18.5 all_gather.55
  85.5 15.4 all_gather.52
  151.2 242.0 %all-gather.17.cloned.1.call-done = bf16[1536,8960]{1,0:T(8,128)(2,1)} async-done(((bf16[384,8960]{1,0:T(8,128)(2,1)}), bf16[1536,8960]{1,0:T(8,128)(2,1)}) %all-gather.17.cloned.1.call-update) | async-done | bytes 27525136 | tf_op jit(solution)/shard_map/all_gather | solution.py:179
  393.2 17.4 fusion.71
  410.6 231.5 %all-gather.15.cloned.1.call-done = bf16[1536,8960]{1,0:T(8,128)(2,1)} async-done(((bf16[384,8960]{1,0:T(8,128)(2,1)}), bf16[1536,8960]{1,0:T(8,128)(2,1)}) %all-gather.15.cloned.1.call-update) | async-done | bytes 27525136 | tf_op jit(solution)/shard_map/all_gather | solution.py:178
  642.1 17.7 fusion.70
  659.8 231.2 %all-gather.19.cloned.1.call-done = bf16[8960,1536]{1,0:T(8,128)(2,1)} async-done(((bf16[2240,1536]{1,0:T(8,128)(2,1)}), bf16[8960,1536]{1,0:T(8,128)(2,1)}) %all-gather.19.cloned.1.call-update) | async-done | bytes 27525136 | tf_op jit(solution)/shard_map/all_gather | solution.py:188
  890.9 24.7 multiply_convert_fusion
  915.6 16.4 fusion.72
  932.1 17.3 multiply_reduce_fusion
  1039.8 14.6 copy.135
  1054.5 22.5 convolution_convert_fusion.2
  1077.0 21.5 convolution_convert_fusion
  1098.5 21.1 convolution_convert_fusion.1
  1119.6 37.6 %pad_maximum_fusion = bf16[1536,17920]{1,0:T(8,128)(2,1)} fusion(bf16[1536,8960]{1,0:T(8,128)(2,1)} %convolution_convert_fusion, bf16[1536,8960]{1,0:T(8,128)(2,1)} %convolution_convert_fusion.1), kind=kLoop, calls=%fused_computation | loop fusion | flops 110100480 | bytes 110100480 | tf_op jit(solution)/shard_map/concatenate | solution.py:203
  1167.2 239.4 %reduce-scatter.11.cloned.1.call-done = bf16[2240,1536]{1,0:T(8,128)(2,1)} async-done(((bf16[8960,1536]{1,0:T(8,128)(2,1)}), bf16[2240,1536]{1,0:T(8,128)(2,1)}) %reduce-scatter.11.cloned.1.call-update) | async-done | bytes 6881296 | tf_op jit(solution)/shard_map/reduce_scatter | solution.py:191
  1406.5 465.6 %reduce-scatter.9.cloned.1.call-done = bf16[384,17920]{1,0:T(8,128)(2,1)} async-done(((bf16[1536,17920]{1,0:T(8,128)(2,1)}), bf16[384,17920]{1,0:T(8,128)(2,1)}) %reduce-scatter.9.cloned.1.call-update) | async-done | bytes 13762576 | tf_op jit(solution)/shard_map/reduce_scatter | solution.py:202
  1886.0 18.2 convolution_add_fusion.3
  1907.5 15.8 all-reduce.7
  1923.6 15.1 all-reduce.8
  1944.8 123.6 %all-gather.21.cloned.1.call-done = bf16[3072,3584]{0,1:T(8,128)(2,1)} async-done(((bf16[384,3584]{0,1:T(8,128)(2,1)}), bf16[3072,3584]{0,1:T(8,128)(2,1)}) %all-gather.21.cloned.1.call-update) | async-done | bytes 22020112 | tf_op jit(solution)/shard_map/all_gather | solution.py:305
  2068.4 21.2 copy.140
  2089.6 23.0 bitcast_reduce_fusion
  2122.1 354.3 %all-reduce.13.cloned.1.call-done = (bf16[384,17920]{1,0:T(8,128)(2,1)}, bf16[2240,1536]{1,0:T(8,128)(2,1)}) async-done(((bf16[384,17920]{1,0:T(8,128)(2,1)}, bf16[2240,1536]{1,0:T(8,128)(2,1)}), (bf16[384,17920]{1,0:T(8,128)(2,1)}, bf16[2240,1536]{1,0:T(8,128)(2,1)})) %all-reduce.13.cloned.1.call-update) | async-done | bytes 20643856 | tf_op jit(solution)/shard_map/psum | solution.py:306
  (263 shorter events, 261.2 us)
Async XLA Ops:
  7.2 110.5 %all-gather.11.cloned.1.call-start = ((), (), s32[]{:S(2)}) async-start(), calls=%async_computation.4 | async-start | bytes 5898240 | tf_op jit(solution)/shard_map/all_gather | solution.py:116
  7.9 138.5 %all-gather.13.cloned.1.call-start = ((), (), s32[]{:S(2)}) async-start(), calls=%async_computation.5 | async-start | bytes 5898240 | tf_op jit(solution)/shard_map/all_gather | solution.py:119
  8.7 384.5 %all-gather.17.cloned.1.call-start = ((), (), s32[]{:S(2)}) async-start(), calls=%async_computation.7 | async-start | bytes 34406400 | tf_op jit(solution)/shard_map/all_gather | solution.py:179
  9.4 632.7 %all-gather.15.cloned.1.call-start = ((), (), s32[]{:S(2)}) async-start(), calls=%async_computation.6 | async-start | bytes 34406400 | tf_op jit(solution)/shard_map/all_gather | solution.py:178
  10.0 37.0 %copy-start.54 = (s32[1,8]{1,0:T(1,128)S(1)}, s32[1,8]{1,0:T(1,128)}, u32[]{:S(2)}) copy-start(s32[1,8]{1,0:T(1,128)} %param.18) | copy-start | bytes 100
  10.1 39.7 %copy-start.39 = (bf16[384,256]{1,0:T(8,128)(2,1)S(1)}, bf16[384,256]{1,0:T(8,128)(2,1)}, u32[]{:S(2)}) copy-start(bf16[384,256]{1,0:T(8,128)(2,1)} %param.22) | copy-start | bytes 589828
  10.1 880.9 %all-gather.19.cloned.1.call-start = ((), (), s32[]{:S(2)}) async-start(), calls=%async_computation.8 | async-start | bytes 34406400 | tf_op jit(solution)/shard_map/all_gather | solution.py:188
  10.6 57.6 %copy-start.5 = (bf16[320,1536]{1,0:T(8,128)(2,1)S(1)}, bf16[320,1536]{1,0:T(8,128)(2,1)}, u32[]{:S(2)}) copy-start(bf16[320,1536]{1,0:T(8,128)(2,1)} %param.16) | copy-start | bytes 2949124
  10.7 1014.3 %reduce-scatter.7.cloned.1.call-start = ((), (), s32[]{:S(2)}) async-start(), calls=%async_computation.9 | async-start | bytes 1638400 | tf_op jit(solution)/shard_map/reduce_scatter | solution.py:243
  39.1 78.5 %copy-start.41 = (f32[1536]{0:T(1024)}, f32[1536]{0:T(1024)S(1)}, u32[]{:S(2)}) copy-start(f32[1536]{0:T(1024)S(1)} %reshape.340) | copy-start | bytes 18436
  48.7 21.5 copy-start.25
  48.9 76.8 %copy-start.28 = (f32[320,128]{0,1:T(8,128)}, f32[320,128]{0,1:T(8,128)S(1)}, u32[]{:S(2)}) copy-start(f32[320,128]{0,1:T(8,128)S(1)} %copy.90) | copy-start | bytes 491524
  69.2 48.5 %copy-start.43 = (f32[320]{0:T(512)}, f32[320]{0:T(512)S(1)}, u32[]{:S(2)}) copy-start(f32[320]{0:T(512)S(1)} %add_rsqrt_fusion.1) | copy-start | bytes 3844
  150.9 798.5 %copy-start.3 = (f32[320,1536]{1,0:T(8,128)}, f32[320,1536]{1,0:T(8,128)S(1)}, u32[]{:S(2)}) copy-start(f32[320,1536]{1,0:T(8,128)S(1)} %get-tuple-element.90) | copy-start | bytes 5898244
  151.2 242.0 %copy-start.36 = (bf16[320,1536]{1,0:T(8,128)(2,1)}, bf16[320,1536]{1,0:T(8,128)(2,1)S(1)}, u32[]{:S(2)}) copy-start(bf16[320,1536]{1,0:T(8,128)(2,1)S(1)} %multiply_convert_fusion.3) | copy-start | bytes 2949124
  410.6 480.4 %copy-start.35 = (bf16[320,1536]{1,0:T(8,128)(2,1)S(1)}, bf16[320,1536]{1,0:T(8,128)(2,1)}, u32[]{:S(2)}) copy-start(bf16[320,1536]{1,0:T(8,128)(2,1)} %param.17) | copy-start | bytes 2949124
  915.6 37.1 %slice-start = ((s8[4718592]{0:T(1024)(128)(4,1)}), s8[4194304]{0:T(1024)(128)(4,1)S(1)}, s32[]{:S(2)}) async-start(s8[4718592]{0:T(1024)(128)(4,1)} %bitcast.137), calls=%async_computation.15 | async-start | bytes 8388608
  995.5 166.9 %reduce-scatter.13.cloned.1.call-start = ((), (), s32[]{:S(2)}) async-start(), calls=%async_computation.13 | async-start | bytes 13762560
  1054.4 352.1 %reduce-scatter.11.cloned.1.call-start = ((), (), s32[]{:S(2)}) async-start(), calls=%async_computation.11 | async-start | bytes 34406400 | tf_op jit(solution)/shard_map/reduce_scatter | solution.py:191
  1076.9 795.2 %reduce-scatter.9.cloned.1.call-start = ((), (), s32[]{:S(2)}) async-start(), calls=%async_computation.10 | async-start | bytes 68812800 | tf_op jit(solution)/shard_map/reduce_scatter | solution.py:202
  1077.0 21.5 copy-start.37
  1157.2 911.2 %all-gather.21.cloned.1.call-start = ((), (), s32[]{:S(2)}) async-start(), calls=%async_computation.12 | async-start | bytes 24772608 | tf_op jit(solution)/shard_map/all_gather | solution.py:305
  1166.9 1309.5 %all-reduce.13.cloned.1.call-start = ((), (), s32[]{:S(2)}) async-start(), calls=%async_computation.14 | async-start | bytes 41287680 | tf_op jit(solution)/shard_map/psum | solution.py:306
  1905.4 36.0 %copy-start.12 = (f32[320,1536]{1,0:T(8,128)S(1)}, f32[320,1536]{1,0:T(8,128)}, u32[]{:S(2)}) copy-start(f32[320,1536]{1,0:T(8,128)} %copy-done.10) | copy-start | bytes 5898244
  (46 other events, 249.5 us)
Sparse Core Ops, SparseCore 0:
  9.9 69.6 all-gather.10
  81.4 62.6 all-gather.12
  146.0 247.1 all-gather.16
  394.9 247.1 all-gather.14
  643.8 247.1 all-gather.18
  995.6 29.3 reduce-scatter.6
  1054.5 107.8 reduce-scatter.12
  1165.5 240.9 reduce-scatter.10
  1409.9 462.1 reduce-scatter.8
  1874.2 194.1 all-gather.20
  2071.0 405.2 all-reduce.12
